TPU v7x, 256 devices: a whole 4x4x8 slice. The times are simulated.
256 devices in a mesh: expert: 64 (over z, y, core), dp: 4 (over x).
Axes of the slice: x: 4, y: 4, z: 8, core: 2. Of those that a mesh axis runs over, the one named last changes fastest.
Arguments:
- prenorm_input: bfloat16 [32768, 1280], P(('expert', 'dp')), may hold values from -6 to 6
- gain: float32 [1280], replicated, may hold values from 0.25 to 1.75
- router: bfloat16 [1280, 32], replicated, may hold values from -0.15625 to 0.15625
- routes: int32 [32768, 2], P(('expert', 'dp')), may hold values from 0 to 31, all different within a row; in each aligned block of 128 rows (0 to 127, 128 to 255, ...) at most 10 rows name the same one
- w_in: bfloat16 [64, 1280, 1280], P('expert', None, 'dp'), may hold values from -0.15625 to 0.15625
- w_out: bfloat16 [64, 1280, 1280], P('expert', 'dp'), may hold values from -0.125 to 0.125
- cotangent: bfloat16 [32768, 1280], P(('expert', 'dp')), may hold values from -18 to 18
Outputs:
- input_grad: bfloat16 [32768, 1280], P(('expert', 'dp'))
- grad_in: bfloat16 [64, 1280, 1280], P('expert', None, 'dp')
- grad_out: bfloat16 [64, 1280, 1280], P('expert', 'dp')
- grad_router: float32 [1280, 32], replicated
- grad_gain: float32 [1280], replicated
Inputs may be any that keep to these rules, and one draw needn't show every extreme that they name: `routes`: each row names 2 different experts; among the rows of one device no expert is named more than 10 times.
All inputs are finite; a program needn't handle non-finite values.
Results may differ from a plain program's by a relative error of at most 0.015.
Values may be sent and summed in bfloat16 or wider, within the bound.
A program may use at most 128 MiB of HBM per device.

v0:
```python
import math
import jax
import jax.numpy as jnp
from jax import lax
from jax.sharding import PartitionSpec as P


def gelu_parts(pre):
    coeff = math.sqrt(2.0 / math.pi)
    inner = coeff * (pre + 0.044715 * pre * pre * pre)
    tanh_val = jnp.tanh(inner)
    value = 0.5 * pre * (1.0 + tanh_val)
    slope = 0.5 * (1.0 + tanh_val) + 0.5 * pre * (1.0 - tanh_val * tanh_val) * coeff * (
        1.0 + 3.0 * 0.044715 * pre * pre
    )
    return (value, slope)


def norm_pieces(block, gain):
    values = block.astype(jnp.float32)
    centred_rows = values - jnp.mean(values, axis=1, keepdims=True)
    inverse_deviation = lax.rsqrt(
        jnp.mean(centred_rows * centred_rows, axis=1, keepdims=True) + 1e-06
    )
    normalized_rows = centred_rows * inverse_deviation
    return (
        normalized_rows,
        inverse_deviation,
        (normalized_rows * gain[None, :]).astype(jnp.bfloat16),
    )


def slot_index(routing_rows, expert_list, expert_capacity):
    flat = routing_rows.reshape(-1)
    onehot = (flat[:, None] == jnp.arange(expert_list, dtype=jnp.int32)[None, :]).astype(jnp.int32)
    before = jnp.cumsum(onehot, axis=0) - onehot
    slot = jnp.sum(before * onehot, axis=1)
    return flat * expert_capacity + slot


def expert_pass(rows_m, rows_d, column, w_first, w_second):
    gate = jax.nn.sigmoid(jnp.dot(rows_m, column, preferred_element_type=jnp.float32)[:, 0])
    pre = jnp.dot(rows_m, w_first, preferred_element_type=jnp.float32)
    value, slope = gelu_parts(pre)
    hidden = value.astype(jnp.bfloat16)
    back = jnp.dot(rows_d, w_second.T, preferred_element_type=jnp.float32)
    gate_gradient = jnp.sum(hidden.astype(jnp.float32) * back, axis=1)
    grad_pre = (gate[:, None] * back * slope).astype(jnp.bfloat16)
    grad_y = (gate[:, None] * rows_d.astype(jnp.float32)).astype(jnp.bfloat16)
    grad_second = jnp.dot(hidden.T, grad_y, preferred_element_type=jnp.float32)
    grad_first = jnp.dot(rows_m.T, grad_pre, preferred_element_type=jnp.float32)
    row_gradient = jnp.dot(grad_pre, w_first.T, preferred_element_type=jnp.float32)
    return (row_gradient, gate_gradient, grad_first, grad_second)


def body(prenorm_input, gain, router, routes, w_in, w_out, cotangent):
    halves = lax.axis_size("expert")
    expert_list = halves // 2
    groups = lax.axis_size("dp")
    tok_rows = prenorm_input.shape[0]
    top = routes.shape[1]
    width = prenorm_input.shape[1]
    expert_capacity = max(2, 5 * tok_rows * top // (4 * expert_list))
    slots = expert_list * expert_capacity
    hi = lax.Precision.HIGHEST
    normalized_rows, inverse_deviation, mixed_rows = norm_pieces(prenorm_input, gain)
    where = slot_index(routes, expert_list, expert_capacity)
    places = (where[None, :] == jnp.arange(slots, dtype=jnp.int32)[:, None]).astype(jnp.bfloat16)
    send_m = jnp.dot(
        places, jnp.repeat(mixed_rows, top, axis=0), preferred_element_type=jnp.float32
    ).astype(jnp.bfloat16)
    send_d = jnp.dot(
        places, jnp.repeat(cotangent, top, axis=0), preferred_element_type=jnp.float32
    ).astype(jnp.bfloat16)
    send_m = jnp.repeat(send_m.reshape(expert_list, expert_capacity, width), 2, axis=0)
    send_d = jnp.repeat(send_d.reshape(expert_list, expert_capacity, width), 2, axis=0)
    recv_m, recv_d = (
        lax.all_to_all(send_m, "expert", split_axis=0, concat_axis=0, tiled=True),
        lax.all_to_all(send_d, "expert", split_axis=0, concat_axis=0, tiled=True),
    )
    own = lax.axis_index("expert") // 2
    column = lax.dynamic_slice_in_dim(router, own, 1, 1)
    all_m, all_d = (
        lax.all_gather(recv_m[None], "dp", axis=0, tiled=True),
        lax.all_gather(recv_d[None], "dp", axis=0, tiled=True),
    )
    row_gradient, gate_gradient, grad_first, grad_second = expert_pass(
        all_m.reshape(-1, width), all_d.reshape(-1, width), column, w_in[0], w_out[0]
    )
    summed_rows, summed_gate = (
        lax.psum_scatter(
            row_gradient.reshape(groups, halves * expert_capacity, width).astype(jnp.bfloat16),
            "dp",
            scatter_dimension=0,
            tiled=True,
        ).astype(jnp.float32),
        lax.psum_scatter(
            gate_gradient.reshape(groups, halves * expert_capacity).astype(jnp.bfloat16),
            "dp",
            scatter_dimension=0,
            tiled=True,
        ).astype(jnp.float32),
    )
    back_rows = summed_rows[0].reshape(halves, expert_capacity, width)
    back_gate = summed_gate[0].reshape(halves, expert_capacity)
    grad_in = grad_first[None].astype(jnp.bfloat16)
    grad_out = grad_second[None].astype(jnp.bfloat16)
    ret_rows, ret_gate = (
        lax.all_to_all(
            back_rows.astype(jnp.bfloat16), "expert", split_axis=0, concat_axis=0, tiled=True
        ).astype(back_rows.dtype),
        lax.all_to_all(
            back_gate.astype(jnp.bfloat16), "expert", split_axis=0, concat_axis=0, tiled=True
        ).astype(back_gate.dtype),
    )
    pair_rows = jnp.sum(ret_rows.reshape(expert_list, 2, expert_capacity, width), axis=1).reshape(
        slots, width
    )
    pair_gate = jnp.sum(ret_gate.reshape(expert_list, 2, expert_capacity), axis=1).reshape(slots)
    grad_expert = jnp.sum(jnp.take(pair_rows, where, axis=0).reshape(tok_rows, top, width), axis=1)
    dgate_tok = jnp.take(pair_gate, where, axis=0).reshape(tok_rows, top)
    logits = jnp.dot(mixed_rows, router, preferred_element_type=jnp.float32)
    choose = (routes[:, :, None] == jnp.arange(expert_list, dtype=jnp.int32)[None, None, :]).astype(
        jnp.float32
    )
    gates = jax.nn.sigmoid(jnp.sum(choose * logits[:, None, :], axis=2))
    dlogit = jnp.sum(choose * (dgate_tok * gates * (1.0 - gates))[:, :, None], axis=1)
    mixed_gradient = grad_expert + jnp.dot(dlogit, router.astype(jnp.float32).T, precision=hi)
    router_term = jnp.dot(mixed_rows.astype(jnp.float32).T, dlogit, precision=hi)
    gain_product = jnp.sum(mixed_gradient * normalized_rows, axis=0)
    grad_router, grad_gain = lax.psum((router_term, gain_product), ("expert", "dp"))
    scaled_rows = mixed_gradient * gain[None, :]
    mean_first_term = jnp.mean(scaled_rows, axis=1, keepdims=True)
    mean_second_term = jnp.mean(scaled_rows * normalized_rows, axis=1, keepdims=True)
    norm_backward = inverse_deviation * (
        scaled_rows - mean_first_term - normalized_rows * mean_second_term
    )
    input_grad = (cotangent.astype(jnp.float32) + norm_backward).astype(jnp.bfloat16)
    return (input_grad, grad_in, grad_out, grad_router, grad_gain)


def solution(mesh):
    in_specs = (
        P(("expert", "dp"), None),
        P(),
        P(),
        P(("expert", "dp"), None),
        P("expert", None, "dp"),
        P("expert", "dp", None),
        P(("expert", "dp"), None),
    )
    out_specs = (
        P(("expert", "dp"), None),
        P("expert", None, "dp"),
        P("expert", "dp", None),
        P(),
        P(),
    )
    return jax.shard_map(body, mesh=mesh, in_specs=in_specs, out_specs=out_specs, check_vma=False)
```

profile of v0, /device:TPU:1, one launch (start us, length us, event | category | flops | bytes accessed | tf_op | source)
XLA Modules:
  0.0 642.1 jit_solution(16606466589608056609)
XLA Ops:
  7.2 0.9 copy.48
  9.3 1.1 convert_reduce_fusion.1
  10.4 1.2 fusion.32
  11.6 1.2 fusion.25
  15.1 75.7 %all_to_all.21 = bf16[64,10,1280]{2,1,0:T(8,128)(2,1)S(1)} all-to-all(bf16[64,10,1280]{2,1,0:T(8,128)(2,1)S(1)} %bitcast.60), channel_id=1, replica_groups=mesh['expert'=64,'dp'=4] {'expert'}, dimensions={0} | all-to-all | bytes 3276800 | tf_op jit(solution)/shard_map/all_to_all | solution.py:78
  90.8 1.7 copy.53
  94.1 68.1 %all_to_all.22 = bf16[64,10,1280]{2,1,0:T(8,128)(2,1)S(1)} all-to-all(bf16[64,10,1280]{2,1,0:T(8,128)(2,1)S(1)} %bitcast.61), channel_id=1, replica_groups=mesh['expert'=64,'dp'=4] {'expert'}, dimensions={0} | all-to-all | bytes 3276800 | tf_op jit(solution)/shard_map/all_to_all | solution.py:79
  162.2 1.6 copy.55
  163.9 11.2 %copy.54 = bf16[256,10,1280]{2,1,0:T(8,128)(2,1)} copy(bf16[256,10,1280]{2,0,1:T(8,128)(2,1)} %all-gather.5.cloned.1.call-done) | data formatting | bytes 13107200 | tf_op jit(solution)/shard_map/all_gather | solution.py:84
  175.2 13.0 %reshape.183 = bf16[2560,1280]{1,0:T(8,128)(2,1)} reshape(bf16[256,10,1280]{2,1,0:T(8,128)(2,1)} %copy.54) | data formatting | bytes 13107200 | tf_op jit(solution)/shard_map/reshape | solution.py:88
  188.2 4.9 convolution_reduce_fusion
  193.2 4.1 fusion.15
  197.2 34.7 %all-gather.7.cloned.1.call-done = bf16[256,10,1280]{2,0,1:T(8,128)(2,1)} async-done(((bf16[64,10,1280]{2,0,1:T(8,128)(2,1)}), bf16[256,10,1280]{2,0,1:T(8,128)(2,1)}) %all-gather.7.cloned.1.call-update) | async-done | bytes 6553616 | tf_op jit(solution)/shard_map/all_gather | solution.py:85
  231.9 10.8 %copy.56 = bf16[256,10,1280]{2,1,0:T(8,128)(2,1)} copy(bf16[256,10,1280]{2,0,1:T(8,128)(2,1)} %all-gather.7.cloned.1.call-done) | data formatting | bytes 13107200 | tf_op jit(solution)/shard_map/all_gather | solution.py:85
  242.8 12.8 %reshape.188 = bf16[2560,1280]{1,0:T(8,128)(2,1)} reshape(bf16[256,10,1280]{2,1,0:T(8,128)(2,1)} %copy.56) | data formatting | bytes 13107200 | tf_op jit(solution)/shard_map/reshape | solution.py:88
  255.6 8.9 %multiply_reduce_fusion = (bf16[2560]{0:T(1024)(128)(2,1)S(1)}, bf16[2560,320]{0,1:T(8,128)(2,1)S(1)}) fusion(f32[2560,320]{0,1:T(8,128)} %fusion.15, f32[2560]{0:T(1024)S(1)} %add_divide_fusion, bf16[2560,1280]{1,0:T(8,128)(2,1)} %reshape.188, bf16[1,320,1280]{2,1,0:T(8,128)(2,1)S(1)} %copy-done.14), kind=kOutput, calls=%fused_computation.16 | convolution fusion | flops 2117629440 | bytes 12303360 | tf_op jit(solution)/shard_map/dot_general | solution.py:46
  264.6 5.6 convolution_convert_fusion
  271.4 7.0 %all-reduce = bf16[4,640]{1,0:T(4,128)(2,1)S(1)} all-reduce(bf16[4,640]{1,0:T(4,128)(2,1)S(1)} %convert_element_type.107), channel_id=5, replica_groups=mesh['expert'=64,'dp'=4] {'dp'}, use_global_device_ids=true, to_apply=%region_9.10.clone | all-reduce | flops 2560 | bytes 10240
  279.1 0.8 convert_element_type.119
  279.9 13.2 %all-to-all-start.3 = ((bf16[64,1,10]{2,1,0:T(2,128)(2,1)}), bf16[64,1,10]{2,1,0:T(2,128)(2,1)S(1)}, u32[]{:S(2)}, u32[]{:S(2)}) async-start(bf16[64,1,10]{2,1,0:T(2,128)(2,1)} %convert_element_type.119), calls=%async_computation.4 | async-start | bytes 65536 | tf_op jit(solution)/shard_map/all_to_all | solution.py:112
  293.1 46.7 %reduce-scatter.2.cloned.1.call-done = bf16[1,640,1280]{2,1,0:T(8,128)(2,1)} async-done(((bf16[4,640,1280]{2,1,0:T(8,128)(2,1)}), bf16[1,640,1280]{2,1,0:T(8,128)(2,1)}) %reduce-scatter.2.cloned.1.call-update) | async-done | bytes 1638416 | tf_op jit(solution)/shard_map/reduce_scatter | solution.py:91
  339.8 4.0 convert_element_type.103
  344.4 10.7 %all-to-all-start.2 = ((bf16[64,10,1280]{2,1,0:T(8,128)(2,1)}), bf16[64,10,1280]{2,1,0:T(8,128)(2,1)S(1)}, u32[]{:S(2)}, u32[]{:S(2)}) async-start(bf16[64,10,1280]{2,1,0:T(8,128)(2,1)} %convert_element_type.103), calls=%async_computation.3 | async-start | bytes 5242880 | tf_op jit(solution)/shard_map/all_to_all | solution.py:109
  355.2 0.8 reduce_sum.115
  356.0 0.7 copy.58
  356.7 1.0 mul.193
  357.7 1.4 copy.51
  359.1 1.1 fusion.41
  360.9 6.7 %fusion.10 = bf16[1,1280,320]{1,2,0:T(8,128)(2,1)} fusion(bf16[2560,320]{0,1:T(8,128)(2,1)} %copy-done.15, bf16[2560,1280]{1,0:T(8,128)(2,1)} %reshape.183), kind=kOutput, calls=%fused_computation.22 | convolution fusion | flops 2097561600 | bytes 9011200 | tf_op jit(solution)/shard_map/dot_general | solution.py:51
  367.6 6.9 %fusion.11 = bf16[1,320,1280]{2,1,0:T(8,128)(2,1)} fusion(bf16[2560,1280]{1,0:T(8,128)(2,1)} %reshape.188, f32[2560]{0:T(1024)S(1)} %add_divide_fusion, f32[2560,320]{0,1:T(8,128)S(1)} %copy-done.17), kind=kOutput, calls=%fused_computation.23 | convolution fusion | flops 2114764800 | bytes 10659840 | tf_op jit(solution)/shard_map/dot_general | solution.py:50
  375.2 0.8 reduce_sum.120
  376.1 2.2 gather_fusion.1
  378.3 0.8 gather.15
  379.1 0.9 copy.60
  380.0 1.3 subtract_multiply_fusion
  381.3 0.7 copy.52
  382.7 1.9 fusion.42
  384.6 31.6 %all-to-all-done.2 = bf16[64,10,1280]{2,1,0:T(8,128)(2,1)S(1)} async-done(((bf16[64,10,1280]{2,1,0:T(8,128)(2,1)}), bf16[64,10,1280]{2,1,0:T(8,128)(2,1)S(1)}, u32[]{:S(2)}, u32[]{:S(2)}) %all-to-all-start.2) | async-done | bytes 1638432 | tf_op jit(solution)/shard_map/all_to_all | solution.py:109
  416.2 2.0 convert_reduce_fusion
  418.2 1.9 reshape.191
  420.1 2.2 gather_fusion
  422.3 2.1 gather.13
  424.5 1.7 select_reduce_fusion
  426.2 0.7 fusion.31
  427.0 1.0 fusion.30
  428.0 75.6 %psum.15 = f32[1280]{0:T(1024)} all-reduce(f32[1280]{0:T(1024)S(1)} %get-tuple-element.5), channel_id=1, replica_groups=mesh['expert'=64,'dp'=4] {'expert','dp'}, use_global_device_ids=true, to_apply=%region_17.18 | all-reduce | flops 1280 | bytes 10240 | tf_op jit(solution)/shard_map/psum | solution.py:131
  503.6 130.3 %all-reduce.3.cloned.1.call-done = f32[1280,32]{0,1:T(8,128)} async-done(((f32[1280,32]{0,1:T(8,128)}), f32[1280,32]{0,1:T(8,128)}) %all-reduce.3.cloned.1.call-update) | async-done | bytes 163856 | tf_op jit(solution)/shard_map/psum | solution.py:131
  634.0 1.6 copy.69
  (79 shorter events, 9.9 us)
Async XLA Ops:
  7.2 186.0 %copy-start = (bf16[1,1280,320]{1,2,0:T(8,128)(2,1)S(1)}, bf16[1,1280,320]{1,2,0:T(8,128)(2,1)}, u32[]{:S(2)}) copy-start(bf16[1,1280,320]{1,2,0:T(8,128)(2,1)} %param.11) | copy-start | bytes 2457604
  7.2 156.7 %all-gather.5.cloned.1.call-start = ((), (), s32[]{:S(2)}) async-start(), calls=%async_computation.7 | async-start | bytes 8192000 | tf_op jit(solution)/shard_map/all_gather | solution.py:84
  11.6 3.3 copy-start.12
  12.9 0.7 copy-start.3
  90.8 1.7 copy-start.4
  92.5 139.5 %all-gather.7.cloned.1.call-start = ((), (), s32[]{:S(2)}) async-start(), calls=%async_computation.8 | async-start | bytes 8192000 | tf_op jit(solution)/shard_map/all_gather | solution.py:85
  163.8 176.0 %reduce-scatter.2.cloned.1.call-start = ((), (), s32[]{:S(2)}) async-start(), calls=%async_computation.5 | async-start | bytes 8192000 | tf_op jit(solution)/shard_map/reduce_scatter | solution.py:91
  175.2 13.0 %copy-start.6 = (bf16[1280,32]{0,1:T(8,128)(2,1)S(1)}, bf16[1280,32]{0,1:T(8,128)(2,1)}, u32[]{:S(2)}) copy-start(bf16[1280,32]{0,1:T(8,128)(2,1)} %param.9) | copy-start | bytes 245764
  188.2 5.0 copy-start.1
  242.8 12.8 %copy-start.14 = (bf16[1,320,1280]{2,1,0:T(8,128)(2,1)S(1)}, bf16[1,320,1280]{2,1,0:T(8,128)(2,1)}, u32[]{:S(2)}) copy-start(bf16[1,320,1280]{2,1,0:T(8,128)(2,1)} %param.12) | copy-start | bytes 2457604
  264.6 5.6 copy-start.15
  270.1 0.7 copy-start.16
  279.9 63.9 %all-to-all-start.3 = ((bf16[64,1,10]{2,1,0:T(2,128)(2,1)}), bf16[64,1,10]{2,1,0:T(2,128)(2,1)S(1)}, u32[]{:S(2)}, u32[]{:S(2)}) async-start(bf16[64,1,10]{2,1,0:T(2,128)(2,1)} %convert_element_type.119), calls=%async_computation.4 | async-start | bytes 65536 | tf_op jit(solution)/shard_map/all_to_all | solution.py:112
  343.8 12.2 %copy-start.11 = (s32[128,2]{0,1:T(2,128)S(1)}, s32[128,2]{0,1:T(2,128)}, u32[]{:S(2)}) copy-start(s32[128,2]{0,1:T(2,128)} %param.10) | copy-start | bytes 3076
  343.8 0.6 copy-start.7
  344.4 71.8 %all-to-all-start.2 = ((bf16[64,10,1280]{2,1,0:T(8,128)(2,1)}), bf16[64,10,1280]{2,1,0:T(8,128)(2,1)S(1)}, u32[]{:S(2)}, u32[]{:S(2)}) async-start(bf16[64,10,1280]{2,1,0:T(8,128)(2,1)} %convert_element_type.103), calls=%async_computation.3 | async-start | bytes 5242880 | tf_op jit(solution)/shard_map/all_to_all | solution.py:109
  355.1 278.8 %all-reduce.3.cloned.1.call-start = ((), (), s32[]{:S(2)}) async-start(), calls=%async_computation.6 | async-start | bytes 327680 | tf_op jit(solution)/shard_map/psum | solution.py:131
  360.9 6.7 %copy-start.17 = (f32[2560,320]{0,1:T(8,128)S(1)}, f32[2560,320]{0,1:T(8,128)}, u32[]{:S(2)}) copy-start(f32[2560,320]{0,1:T(8,128)} %fusion.15) | copy-start | bytes 9830404
  367.6 6.9 %copy-start.8 = (bf16[64,1,10]{2,1,0:T(2,128)(2,1)S(1)}, bf16[64,1,10]{2,1,0:T(2,128)(2,1)}, u32[]{:S(2)}) copy-start(bf16[64,1,10]{2,1,0:T(2,128)(2,1)} %copy-done.7) | copy-start | bytes 3844
  420.1 4.4 copy-start.10
  422.3 3.9 copy-start.2
  422.3 3.9 copy-start.9
  422.3 3.9 copy-start.13
  422.3 4.6 copy-start.5
Sparse Core Ops, SparseCore 0:
  92.6 66.4 all-gather.4
  164.0 67.9 all-gather.6
  270.3 69.4 reduce-scatter.1
  384.7 249.2 all-reduce.2
where the time goes:
time: 644 us; the launch traced here: 642 us
  waiting for transfers between devices  243 us (38%)
  blocking collectives  226 us (35%)
  local copies, waits for them, and re-layouts  79.3 us (12%)
  matrix products  41.6 us (6%)
  starting transfers between devices  24.1 us (4%)
  between operations  14.1 us (2%)
  other arithmetic  13.1 us (2%)
    psum x1, waiting for transfers between devices, body(): lax.psum((router_term, gain_product), ('expert', 'dp'))  130 us
    all_to_all x1, blocking collectives, body(): lax.all_to_all(send_m, 'expert', split_axis=0, concat_axis=0, tiled=True)  75.7 us
    psum x1, blocking collectives, body(): lax.psum((router_term, gain_product), ('expert', 'dp'))  75.6 us
    all_to_all x1, blocking collectives, body(): lax.all_to_all(send_d, 'expert', split_axis=0, concat_axis=0, tiled=True)  68.1 us
    reduce_scatter x1, waiting for transfers between devices, body(): lax.psum_scatter(row_gradient.reshape(groups, halves * expert_capacity, w...  46.7 us
    all_gather x1, waiting for transfers between devices, body(): lax.all_gather(recv_d[None], 'dp', axis=0, tiled=True)  34.7 us
    all_to_all x1, waiting for transfers between devices, body(): lax.all_to_all(back_rows.astype(jnp.bfloat16), 'expert', split_axis=0, co...  31.6 us
    all_to_all x1, starting transfers between devices, body(): lax.all_to_all(back_gate.astype(jnp.bfloat16), 'expert', split_axis=0, co...  13.2 us
  transfers between devices with their start and end apart: 6, of which 4 were waited for; matrix products, arithmetic and copies ran while one was open for 13% of the time, Pallas kernels for 0%

commit v1 on v0

--- a/solution.py
+++ b/solution.py
@@ -82,7 +82,9 @@
     column = lax.dynamic_slice_in_dim(router, own, 1, 1)
     all_m, all_d = (
         lax.all_gather(recv_m[None], "dp", axis=0, tiled=True),
-        lax.all_gather(recv_d[None], "dp", axis=0, tiled=True),
+        jnp.concatenate(
+            lax.all_to_all(jnp.stack([recv_d[None]] * lax.axis_size("dp")), "dp", 0, 0), axis=0
+        ),
     )
     row_gradient, gate_gradient, grad_first, grad_second = expert_pass(
         all_m.reshape(-1, width), all_d.reshape(-1, width), column, w_in[0], w_out[0]

time: 644 us -> 687 us (1.067); the launches traced: 642 us -> 677 us
  waiting for transfers between devices: 243 us -> 282 us
  matrix products: 41.6 us -> 34.7 us
    all_to_all x0 -> x1, waiting for transfers between devices: none -> 73.9 us  [body(): lax.all_to_all(jnp.stack([recv_d[None]] * lax.axis_size('dp')), 'dp', 0, 0)]
    all_gather x1 -> x0, waiting for transfers between devices: 34.7 us -> none  [body(): lax.all_gather(recv_d[None], 'dp', axis=0, tiled=True)]
    another operation x1 -> x3, local copies, waits for them, and re-layouts: 0.01 us -> 16.5 us  [the longest x1 12.9 us: body(): all_d.reshape(-1, width)]
    reshape x1 -> x0, local copies, waits for them, and re-layouts: 12.8 us -> none  [body(): all_d.reshape(-1, width)]
    all_to_all x0 -> x1, local copies, waits for them, and re-layouts: none -> 10.9 us  [body(): lax.all_to_all(jnp.stack([recv_d[None]] * lax.axis_size('dp')), 'dp', 0, 0)]
    all_gather x1 -> x0, local copies, waits for them, and re-layouts: 10.8 us -> none  [body(): lax.all_gather(recv_d[None], 'dp', axis=0, tiled=True)]
  transfers between devices with their start and end apart: 6 -> 6, of which waited for: 4 -> 4; matrix products, arithmetic and copies ran while one was open for 13% -> 11% of each run, Pallas kernels for 0% -> 0%
where the time goes in v1:
time: 687 us; the launch traced here: 677 us
  waiting for transfers between devices  282 us (41%)
  blocking collectives  226 us (33%)
  local copies, waits for them, and re-layouts  82.2 us (12%)
  matrix products  34.7 us (5%)
  starting transfers between devices  24.3 us (4%)
  between operations  14.6 us (2%)
  other arithmetic  13.2 us (2%)
    psum x1, waiting for transfers between devices, body(): lax.psum((router_term, gain_product), ('expert', 'dp'))  130 us
    all_to_all x1, blocking collectives, body(): lax.all_to_all(send_m, 'expert', split_axis=0, concat_axis=0, tiled=True)  75.7 us
    psum x1, blocking collectives, body(): lax.psum((router_term, gain_product), ('expert', 'dp'))  75.6 us
    all_to_all x1, waiting for transfers between devices, body(): lax.all_to_all(jnp.stack([recv_d[None]] * lax.axis_size('dp')), 'dp', 0, 0)  73.9 us
    all_to_all x1, blocking collectives, body(): lax.all_to_all(send_d, 'expert', split_axis=0, concat_axis=0, tiled=True)  68.1 us
    reduce_scatter x1, waiting for transfers between devices, body(): lax.psum_scatter(row_gradient.reshape(groups, halves * expert_capacity, w...  45.8 us
    all_to_all x1, waiting for transfers between devices, body(): lax.all_to_all(back_rows.astype(jnp.bfloat16), 'expert', split_axis=0, co...  31.7 us
  transfers between devices with their start and end apart: 6, of which 4 were waited for; matrix products, arithmetic and copies ran while one was open for 11% of the time, Pallas kernels for 0%

profile of v1, /device:TPU:1, one launch (start us, length us, event | category | flops | bytes accessed | tf_op | source)
XLA Modules:
  0.0 677.2 jit_solution(9703003714067009764)
XLA Ops:
  7.2 0.9 copy.48
  9.3 1.1 convert_reduce_fusion.1
  10.4 1.2 fusion.32
  11.6 1.2 fusion.25
  15.1 75.7 %all_to_all.26 = bf16[64,10,1280]{2,1,0:T(8,128)(2,1)S(1)} all-to-all(bf16[64,10,1280]{2,1,0:T(8,128)(2,1)S(1)} %bitcast.62), channel_id=1, replica_groups=mesh['expert'=64,'dp'=4] {'expert'}, dimensions={0} | all-to-all | bytes 3276800 | tf_op jit(solution)/shard_map/all_to_all | solution.py:78
  90.8 1.7 copy.53
  94.0 68.1 %all_to_all.27 = bf16[64,10,1280]{2,1,0:T(8,128)(2,1)S(1)} all-to-all(bf16[64,10,1280]{2,1,0:T(8,128)(2,1)S(1)} %bitcast.63), channel_id=1, replica_groups=mesh['expert'=64,'dp'=4] {'expert'}, dimensions={0} | all-to-all | bytes 3276800 | tf_op jit(solution)/shard_map/all_to_all | solution.py:79
  162.6 3.5 stack.3
  166.1 5.3 all-to-all-start.2
  171.5 73.9 %all-to-all-done.2 = bf16[4,1,64,10,1280]{4,2,3,1,0:T(8,128)(2,1)} async-done(((bf16[4,1,64,10,1280]{4,2,3,1,0:T(8,128)(2,1)}), bf16[4,1,64,10,1280]{4,2,3,1,0:T(8,128)(2,1)}, u32[]{:S(2)}, u32[]{:S(2)}) %all-to-all-start.2) | async-done | bytes 6553632 | tf_op jit(solution)/shard_map/all_to_all | solution.py:86
  245.3 10.9 %copy.56 = bf16[4,1,64,10,1280]{4,3,2,0,1:T(8,128)(2,1)} copy(bf16[4,1,64,10,1280]{4,2,3,1,0:T(8,128)(2,1)} %all-to-all-done.2) | data formatting | bytes 13107200 | tf_op jit(solution)/shard_map/all_to_all | solution.py:86
  256.2 12.9 %reshape_reshape.3 = bf16[2560,1280]{1,0:T(8,128)(2,1)} reshape(bf16[4,1,64,10,1280]{4,3,2,0,1:T(8,128)(2,1)} %copy.56) | data formatting | bytes 13107200 | tf_op jit(solution)/shard_map/reshape;reshape | solution.py:90
  269.2 10.8 %copy.54 = bf16[256,10,1280]{2,1,0:T(8,128)(2,1)} copy(bf16[256,10,1280]{2,0,1:T(8,128)(2,1)} %all-gather.3.cloned.1.call-done) | data formatting | bytes 13107200 | tf_op jit(solution)/shard_map/all_gather | solution.py:84
  280.0 12.8 %reshape.182 = bf16[2560,1280]{1,0:T(8,128)(2,1)} reshape(bf16[256,10,1280]{2,1,0:T(8,128)(2,1)} %copy.54) | data formatting | bytes 13107200 | tf_op jit(solution)/shard_map/reshape | solution.py:90
  292.8 4.8 convolution_reduce_fusion
  297.7 2.3 fusion.15
  300.1 4.0 multiply_reduce_fusion
  304.1 1.2 copy-done.15
  305.3 5.5 convolution_convert_fusion
  312.1 7.0 %all-reduce = bf16[4,640]{1,0:T(4,128)(2,1)S(1)} all-reduce(bf16[4,640]{1,0:T(4,128)(2,1)S(1)} %convert_element_type.107), channel_id=4, replica_groups=mesh['expert'=64,'dp'=4] {'dp'}, use_global_device_ids=true, to_apply=%region_9.10.clone | all-reduce | flops 2560 | bytes 10240
  319.7 0.8 convert_element_type.119
  320.5 8.1 %all-to-all-start.4 = ((bf16[64,1,10]{2,1,0:T(2,128)(2,1)}), bf16[64,1,10]{2,1,0:T(2,128)(2,1)S(1)}, u32[]{:S(2)}, u32[]{:S(2)}) async-start(bf16[64,1,10]{2,1,0:T(2,128)(2,1)} %convert_element_type.119), calls=%async_computation.5 | async-start | bytes 65536 | tf_op jit(solution)/shard_map/all_to_all | solution.py:114
  328.6 45.8 %reduce-scatter.2.cloned.1.call-done = bf16[1,640,1280]{2,1,0:T(8,128)(2,1)} async-done(((bf16[4,640,1280]{2,1,0:T(8,128)(2,1)}), bf16[1,640,1280]{2,1,0:T(8,128)(2,1)}) %reduce-scatter.2.cloned.1.call-update) | async-done | bytes 1638416 | tf_op jit(solution)/shard_map/reduce_scatter | solution.py:93
  374.4 4.0 convert_element_type.103
  379.0 10.9 %all-to-all-start.3 = ((bf16[64,10,1280]{2,1,0:T(8,128)(2,1)}), bf16[64,10,1280]{2,1,0:T(8,128)(2,1)S(1)}, u32[]{:S(2)}, u32[]{:S(2)}) async-start(bf16[64,10,1280]{2,1,0:T(8,128)(2,1)} %convert_element_type.103), calls=%async_computation.4 | async-start | bytes 5242880 | tf_op jit(solution)/shard_map/all_to_all | solution.py:111
  389.9 0.8 reduce_sum.115
  390.7 0.7 copy.58
  391.5 1.0 mul.193
  392.4 1.5 copy.51
  394.0 1.1 fusion.41
  395.8 6.7 fusion.10
  402.4 6.9 %fusion.11 = bf16[1,320,1280]{2,1,0:T(8,128)(2,1)} fusion(bf16[2560,1280]{1,0:T(8,128)(2,1)} %reshape_reshape.3, f32[2560]{0:T(1024)S(1)} %add_divide_fusion, f32[2560,320]{0,1:T(8,128)S(1)} %copy-done.18), kind=kOutput, calls=%fused_computation.23 | convolution fusion | flops 2114764800 | bytes 10659840 | tf_op jit(solution)/shard_map/dot_general | solution.py:50
  410.0 0.8 reduce_sum.120
  410.9 1.9 gather_fusion.1
  412.9 0.8 gather.15
  413.6 0.9 copy.60
  414.5 1.3 subtract_multiply_fusion
  417.3 1.9 fusion.42
  419.2 31.7 %all-to-all-done.3 = bf16[64,10,1280]{2,1,0:T(8,128)(2,1)S(1)} async-done(((bf16[64,10,1280]{2,1,0:T(8,128)(2,1)}), bf16[64,10,1280]{2,1,0:T(8,128)(2,1)S(1)}, u32[]{:S(2)}, u32[]{:S(2)}) %all-to-all-start.3) | async-done | bytes 1638432 | tf_op jit(solution)/shard_map/all_to_all | solution.py:111
  450.9 2.0 convert_reduce_fusion
  452.9 1.9 reshape.189
  454.8 2.2 gather_fusion
  457.1 2.1 gather.13
  459.2 1.7 select_reduce_fusion
  461.7 1.0 fusion.30
  462.8 75.6 %psum.15 = f32[1280]{0:T(1024)} all-reduce(f32[1280]{0:T(1024)S(1)} %get-tuple-element.5), channel_id=1, replica_groups=mesh['expert'=64,'dp'=4] {'expert','dp'}, use_global_device_ids=true, to_apply=%region_17.18 | all-reduce | flops 1280 | bytes 10240 | tf_op jit(solution)/shard_map/psum | solution.py:133
  538.3 130.4 %all-reduce.3.cloned.1.call-done = f32[1280,32]{0,1:T(8,128)} async-done(((f32[1280,32]{0,1:T(8,128)}), f32[1280,32]{0,1:T(8,128)}) %all-reduce.3.cloned.1.call-update) | async-done | bytes 163856 | tf_op jit(solution)/shard_map/psum | solution.py:133
  668.7 1.6 copy.69
  (86 shorter events, 11.8 us)
Async XLA Ops:
  7.2 290.5 %copy-start = (bf16[1,1280,320]{1,2,0:T(8,128)(2,1)S(1)}, bf16[1,1280,320]{1,2,0:T(8,128)(2,1)}, u32[]{:S(2)}) copy-start(bf16[1,1280,320]{1,2,0:T(8,128)(2,1)} %param.11) | copy-start | bytes 2457604
  7.2 262.0 %all-gather.3.cloned.1.call-start = ((), (), s32[]{:S(2)}) async-start(), calls=%async_computation.8 | async-start | bytes 8192000 | tf_op jit(solution)/shard_map/all_gather | solution.py:84
  11.6 3.3 copy-start.12
  12.9 0.7 copy-start.3
  90.8 1.7 copy-start.4
  166.1 79.2 %all-to-all-start.2 = ((bf16[4,1,64,10,1280]{4,2,3,1,0:T(8,128)(2,1)}), bf16[4,1,64,10,1280]{4,2,3,1,0:T(8,128)(2,1)}, u32[]{:S(2)}, u32[]{:S(2)}) async-start(bf16[4,1,64,10,1280]{4,2,3,1,0:T(8,128)(2,1)} %stack.3), calls=%async_computation.2 | async-start | bytes 13107200 | tf_op jit(solution)/shard_map/all_to_all | solution.py:86
  171.4 203.0 %reduce-scatter.2.cloned.1.call-start = ((), (), s32[]{:S(2)}) async-start(), calls=%async_computation.6 | async-start | bytes 8192000 | tf_op jit(solution)/shard_map/reduce_scatter | solution.py:93
  280.0 12.8 %copy-start.6 = (bf16[1280,32]{0,1:T(8,128)(2,1)S(1)}, bf16[1280,32]{0,1:T(8,128)(2,1)}, u32[]{:S(2)}) copy-start(bf16[1280,32]{0,1:T(8,128)(2,1)} %param.9) | copy-start | bytes 245764
  292.8 4.9 copy-start.1
  292.8 7.2 %slice-start = ((s8[6553600]{0:T(1024)(128)(4,1)}), s8[4194304]{0:T(1024)(128)(4,1)S(1)}, s32[]{:S(2)}) async-start(s8[6553600]{0:T(1024)(128)(4,1)} %bitcast.64), calls=%async_computation.9 | async-start | bytes 8388608
  297.7 2.4 slice-start.1
  297.7 2.4 copy-start.14
  300.1 4.0 copy-start.17
  304.1 1.2 copy-start.15
  310.8 0.7 copy-start.16
  320.5 57.9 %all-to-all-start.4 = ((bf16[64,1,10]{2,1,0:T(2,128)(2,1)}), bf16[64,1,10]{2,1,0:T(2,128)(2,1)S(1)}, u32[]{:S(2)}, u32[]{:S(2)}) async-start(bf16[64,1,10]{2,1,0:T(2,128)(2,1)} %convert_element_type.119), calls=%async_computation.5 | async-start | bytes 65536 | tf_op jit(solution)/shard_map/all_to_all | solution.py:114
  378.4 12.3 %copy-start.11 = (s32[128,2]{0,1:T(2,128)S(1)}, s32[128,2]{0,1:T(2,128)}, u32[]{:S(2)}) copy-start(s32[128,2]{0,1:T(2,128)} %param.10) | copy-start | bytes 3076
  378.4 0.6 copy-start.7
  379.0 71.9 %all-to-all-start.3 = ((bf16[64,10,1280]{2,1,0:T(8,128)(2,1)}), bf16[64,10,1280]{2,1,0:T(8,128)(2,1)S(1)}, u32[]{:S(2)}, u32[]{:S(2)}) async-start(bf16[64,10,1280]{2,1,0:T(8,128)(2,1)} %convert_element_type.103), calls=%async_computation.4 | async-start | bytes 5242880 | tf_op jit(solution)/shard_map/all_to_all | solution.py:111
  389.9 278.8 %all-reduce.3.cloned.1.call-start = ((), (), s32[]{:S(2)}) async-start(), calls=%async_computation.7 | async-start | bytes 327680 | tf_op jit(solution)/shard_map/psum | solution.py:133
  395.8 6.7 copy-start.18
  402.4 6.9 %copy-start.8 = (bf16[64,1,10]{2,1,0:T(2,128)(2,1)S(1)}, bf16[64,1,10]{2,1,0:T(2,128)(2,1)}, u32[]{:S(2)}) copy-start(bf16[64,1,10]{2,1,0:T(2,128)(2,1)} %copy-done.7) | copy-start | bytes 3844
  454.8 4.4 copy-start.10
  457.1 3.9 copy-start.2
  457.1 3.9 copy-start.9
  457.1 3.9 copy-start.13
  457.1 4.6 copy-start.5
Sparse Core Ops, SparseCore 0:
  92.6 66.4 all-gather.2
  310.9 63.4 reduce-scatter.1
  419.3 249.3 all-reduce.2
